TPU v7x, 32 devices: a whole 2x2x4 slice. The times are simulated.
32 devices in a mesh: band: 8 (over z, y), rep: 4 (over x, core).
Axes of the slice: x: 2, y: 2, z: 4, core: 2. Of those that a mesh axis runs over, the one named last changes fastest.
Arguments:
- embeddings: bfloat16 [128, 4096], P('rep', 'band'), may hold values from -6 to 6
- route: int32 [4096, 1], P('band'), may hold values from 0 to 7; in each aligned block of 512 rows (0 to 511, 512 to 1023, ...) at most 160 rows name the same one
- place: bfloat16 [2, 4096], P(None, 'band'), may hold values from 0 to 1
- scales: float32 [4], replicated, may hold values from 0.25 to 1
- first_weight: bfloat16 [512, 512], replicated, may hold values from -0.25 to 0.25
- first_bias: float32 [512], replicated, may hold values from -3 to 3
- second_weight: bfloat16 [512, 512], replicated, may hold values from -0.25 to 0.25
- out_cotangent: bfloat16 [512, 96, 256], P(None, ('band', 'rep')), may hold values from -6 to 6
Outputs:
- embed_gradient: float32 [128, 4096], P('rep', 'band')
- first_weight_gradient: float32 [512, 512], replicated
- first_bias_gradient: float32 [512], replicated
- second_weight_gradient: float32 [512, 512], replicated
Inputs may be any that keep to these rules, and one draw needn't show every extreme that they name: `route`: within the 512 reports of one feed (aligned blocks of rows), at most 160 name the same band, and in some block exactly 160 do.
All inputs are finite; a program needn't handle non-finite values.
Results may differ from a plain program's by a relative error of at most 0.0063.
Values may be sent and summed in bfloat16 or wider, within the bound.
No kernel may reach another device: no remote copies, remote signals or barrier semaphores. Data moves between devices by JAX's collectives and lax.ppermute only.
A program may use at most 128 MiB of HBM per device.

v0:
```python
import jax
import jax.numpy as jnp
from jax import lax
from jax.sharding import PartitionSpec as P

root_two_pi = 0.7978845608028654
cubic = 0.044715


def padded(cells, sides, width):
    for axis, dim in sides:
        count = lax.axis_size(axis)
        ends = count - 1
        head = lax.slice_in_dim(cells, 0, width, axis=dim)
        tail = lax.slice_in_dim(cells, cells.shape[dim] - width, cells.shape[dim], axis=dim)
        cells = jnp.concatenate(
            [
                lax.ppermute(tail, axis, [(i, (i + 1) % count) for i in range(ends)]),
                cells,
                lax.ppermute(head, axis, [((i + 1) % count, i) for i in range(ends)]),
            ],
            axis=dim,
        )
    return cells


def gelu_value(value):
    inner = root_two_pi * (value + cubic * value * value * value)
    return 0.5 * value * (1.0 + jnp.tanh(inner))


def gelu_slope(value):
    tangent = jnp.tanh(root_two_pi * (value + cubic * value * value * value))
    return 0.5 * (1.0 + tangent) + 0.5 * value * (1.0 - tangent * tangent) * root_two_pi * (
        1.0 + 3.0 * cubic * value * value
    )


def kernel_factors(geometry, block, scales, lat_rows, columns):
    north_fraction = geometry[0]
    east_fraction = geometry[1]
    valid = geometry[2]
    centre_rows = jnp.arange(lat_rows, dtype=jnp.float32) + 0.5
    north_gap = (
        ((1 - block).astype(jnp.float32) * lat_rows)[None, :]
        + centre_rows[:, None]
        - (north_fraction * lat_rows)[None, :]
    )
    east_gap = (jnp.arange(columns, dtype=jnp.float32) + 0.5)[:, None] - (east_fraction * columns)[
        None, :
    ]
    reach = scales * lat_rows
    inverse = 0.5 / (reach * reach)
    row_kernel = (
        jnp.exp(-(north_gap * north_gap)[None] * inverse[:, None, None]) * valid[None, None, :]
    ).astype(jnp.bfloat16)
    column_kernel = jnp.exp(-(east_gap * east_gap)[None] * inverse[:, None, None]).astype(
        jnp.bfloat16
    )
    return (row_kernel, column_kernel)


def splat(embedded, row_kernel, column_kernel):
    channels = embedded.shape[0]
    levels, lat_rows, slots = row_kernel.shape
    columns = column_kernel.shape[1]
    sums = []
    weights = []
    for level in range(levels):
        weighted = (embedded[:, None, :] * row_kernel[level][None]).reshape(
            channels * lat_rows, slots
        )
        sums.append(
            lax.dot_general(
                weighted,
                column_kernel[level],
                (((1,), (1,)), ((), ())),
                preferred_element_type=jnp.float32,
            )
        )
        weights.append(
            lax.dot_general(
                row_kernel[level],
                column_kernel[level],
                (((1,), (1,)), ((), ())),
                preferred_element_type=jnp.float32,
            )
        )
    splatted = jnp.stack(sums).reshape(levels, channels, lat_rows * columns)
    density = jnp.stack(weights).reshape(levels, lat_rows * columns)
    features = (
        (splatted / (density[:, None, :] + 1.0))
        .transpose(1, 0, 2)
        .reshape(channels * levels, lat_rows * columns)
        .astype(jnp.bfloat16)
    )
    return (features, density)


def spread_back(gradient, row_kernel, column_kernel):
    levels, lat_rows, slots = row_kernel.shape
    columns = column_kernel.shape[1]
    channels = gradient.shape[0] // levels
    grid = gradient.reshape(channels, levels, lat_rows * columns)
    total = jnp.zeros((channels, slots), jnp.float32)
    for level in range(levels):
        slab = grid[:, level].reshape(channels * lat_rows, columns)
        along = jnp.dot(slab, column_kernel[level], preferred_element_type=jnp.float32).reshape(
            channels, lat_rows, slots
        )
        total = total + jnp.sum(along * row_kernel[level][None].astype(jnp.float32), axis=1)
    return total


def band_ranks(route_rows, bands):
    owner = route_rows[:, 0]
    onehot = (owner[:, None] == jnp.arange(bands, dtype=jnp.int32)[None, :]).astype(jnp.int32)
    running = jnp.cumsum(onehot, axis=0)
    return (owner, jnp.sum((running - 1) * onehot, axis=1))


def on_device(
    embeddings, route, place, scales, first_weight, first_bias, second_weight, out_cotangent
):
    channels, reports = embeddings.shape
    bands = lax.axis_size("band")
    parts = lax.axis_size("rep")
    quarter = lax.axis_index("rep")
    capacity = max(2, 5 * reports // (2 * bands))
    sub_rows = out_cotangent.shape[1]
    lat_rows = sub_rows * parts
    columns = out_cotangent.shape[2]
    levels = scales.shape[0]
    owner, rank = band_ranks(route, bands)
    packed = jnp.concatenate([embeddings, place, jnp.ones((1, reports), jnp.bfloat16)], axis=0)
    rows = channels + 3
    whole = bands * capacity
    outgoing = jnp.zeros((rows, whole), jnp.bfloat16).at[:, owner * capacity + rank].set(packed)
    arrived = lax.all_to_all(outgoing, "band", split_axis=1, concat_axis=1, tiled=True)
    nearby = padded(arrived, (("band", 1),), whole)
    block = jnp.arange(3 * whole, dtype=jnp.int32) // whole
    geometry = nearby[channels:].astype(jnp.float32)
    row_kernel, column_kernel = kernel_factors(geometry, block, scales, lat_rows, columns)
    features, density = splat(nearby[:channels], row_kernel, column_kernel)
    cotangent = out_cotangent.reshape(out_cotangent.shape[0], sub_rows * columns)
    mine = lax.all_to_all(features, "rep", split_axis=1, concat_axis=0, tiled=True)
    local_density = lax.dynamic_slice_in_dim(
        density.reshape(levels, lat_rows, columns), quarter * sub_rows, sub_rows, 1
    ).reshape(levels, sub_rows * columns)
    preact = (
        lax.dot_general(
            first_weight, mine, (((0,), (0,)), ((), ())), preferred_element_type=jnp.float32
        )
        + first_bias[:, None]
    )
    hidden = gelu_value(preact).astype(jnp.bfloat16)
    pre_gradient = (
        jnp.dot(second_weight, cotangent, preferred_element_type=jnp.float32) * gelu_slope(preact)
    ).astype(jnp.bfloat16)
    first_sum = lax.dot_general(
        mine, pre_gradient, (((1,), (1,)), ((), ())), preferred_element_type=jnp.float32
    )
    second_sum = lax.dot_general(
        hidden, cotangent, (((1,), (1,)), ((), ())), preferred_element_type=jnp.float32
    )
    bias_sum = jnp.sum(pre_gradient.astype(jnp.float32), axis=1)
    feature_gradient = jnp.dot(first_weight, pre_gradient, preferred_element_type=jnp.float32)
    count = sub_rows * columns
    cell_part = (
        (feature_gradient.reshape(-1, levels, count) / (local_density[None] + 1.0))
        .reshape(-1, count)
        .astype(jnp.bfloat16)
    )
    splat_gradient = lax.all_to_all(cell_part, "rep", split_axis=0, concat_axis=1, tiled=True)
    totals = lax.psum((first_sum, second_sum, bias_sum), ("band", "rep"))
    slot_gradient = spread_back(splat_gradient, row_kernel, column_kernel)
    outward = jnp.concatenate([slot_gradient[:, :whole], slot_gradient[:, 2 * whole :]], axis=1)
    returned = padded(outward, (("band", 1),), whole)
    own_total = slot_gradient[:, whole : 2 * whole] + returned[:, :whole] + returned[:, 3 * whole :]
    backward = lax.all_to_all(own_total, "band", split_axis=1, concat_axis=1, tiled=True)
    embed_gradient = backward[:, owner * capacity + rank]
    return (embed_gradient, totals[0], totals[2], totals[1])


def solution(mesh):
    return jax.shard_map(
        on_device,
        mesh=mesh,
        in_specs=(
            P("rep", "band"),
            P("band", None),
            P(None, "band"),
            P(),
            P(),
            P(),
            P(),
            P(None, ("band", "rep"), None),
        ),
        out_specs=(P("rep", "band"), P(), P(), P()),
        check_vma=False,
    )
```

profile of v0, /device:TPU:0, one launch (start us, length us, event | category | flops | bytes accessed | tf_op | source)
XLA Modules:
  0.0 270.7 jit_solution(15781892218511032208)
XLA Ops:
  14.6 7.3 %all-to-all-start = ((bf16[35,8,160]{2,0,1:T(8,128)(2,1)}), bf16[35,8,160]{2,0,1:T(8,128)(2,1)S(1)}, u32[]{:S(2)}, u32[]{:S(2)}) async-start(bf16[35,8,160]{2,0,1:T(8,128)(2,1)} %copy.50), calls=%async_computation | async-start | bytes 327680 | tf_op jit(solution)/shard_map/all_to_all | solution.py:139
  22.6 6.9 %all-to-all-done = bf16[35,8,160]{2,0,1:T(8,128)(2,1)S(1)} async-done(((bf16[35,8,160]{2,0,1:T(8,128)(2,1)}), bf16[35,8,160]{2,0,1:T(8,128)(2,1)S(1)}, u32[]{:S(2)}, u32[]{:S(2)}) %all-to-all-start) | async-done | bytes 89632 | tf_op jit(solution)/shard_map/all_to_all | solution.py:139
  35.8 3.3 %collective-permute-done.1 = bf16[35,1280]{1,0:T(8,128)(2,1)S(1)} collective-permute-done((bf16[35,1280]{1,0:T(8,128)(2,1)S(1)}, bf16[35,1280]{1,0:T(8,128)(2,1)S(1)}, u32[]{:S(2)}, u32[]{:S(2)}) %collective-permute-start.1) | collective-permute-done | bytes 89632 | tf_op jit(solution)/shard_map/ppermute | solution.py:20
  41.2 2.9 %exponential_convert_fusion = bf16[4,256,3840]{2,1,0:T(8,128)(2,1)S(1)} fusion(f32[4]{0:T(128)S(1)} %multiply_divide_fusion, f32[256,3840]{1,0:T(8,128)S(1)} %multiply_negate_fusion), kind=kLoop, calls=%fused_computation.2 | loop fusion | flops 7864320 | bytes 11796496 | tf_op jit(solution)/shard_map/convert_element_type | solution.py:57
  49.2 6.1 %broadcast_multiply_fusion.3 = (bf16[32,12,3840]{2,1,0:T(8,128)(2,1)}, bf16[32,12,3840]{2,1,0:T(8,128)(2,1)}, bf16[32,12,3840]{2,1,0:T(8,128)(2,1)}, bf16[32,12,3840]{2,1,0:T(8,128)(2,1)}) fusion(bf16[12,3840]{1,0:T(8,128)(2,1)S(1)} %copy-done.10, bf16[32,3840]{1,0:T(8,128)(2,1)S(1)} %slice.107, bf16[12,3840]{1,0:T(8,128)(2,1)S(1)} %copy-done.9, ...), kind=kLoop, calls=%fused_computation.33 | loop fusion | flops 5898240 | bytes 12410880 | tf_op jit(solution)/shard_map/mul | solution.py:70
  55.3 3.9 %mul.295 = bf16[384,3840]{1,0:T(8,128)(2,1)S(1)} reshape(bf16[32,12,3840]{2,1,0:T(8,128)(2,1)} %get-tuple-element.39) | data formatting | bytes 5898240 | tf_op jit(solution)/shard_map/mul | solution.py:70
  59.1 3.2 %fusion.18 = f32[384,256]{1,0:T(8,128)} fusion(bf16[384,3840]{1,0:T(8,128)(2,1)S(1)} %mul.295, bf16[4,256,3840]{2,1,0:T(8,128)(2,1)} %copy-done.1), kind=kOutput, calls=%fused_computation.28 | convolution fusion | flops 754974720 | bytes 5308416 | tf_op jit(solution)/shard_map/dot_general | solution.py:74
  64.5 3.9 %mul.306 = bf16[384,3840]{1,0:T(8,128)(2,1)S(1)} reshape(bf16[32,12,3840]{2,1,0:T(8,128)(2,1)} %get-tuple-element.40) | data formatting | bytes 5898240 | tf_op jit(solution)/shard_map/mul | solution.py:70
  68.4 3.2 %fusion.14 = f32[384,256]{1,0:T(8,128)} fusion(bf16[384,3840]{1,0:T(8,128)(2,1)S(1)} %mul.306, bf16[4,256,3840]{2,1,0:T(8,128)(2,1)} %copy-done.1), kind=kOutput, calls=%fused_computation.24 | convolution fusion | flops 754974720 | bytes 5308416 | tf_op jit(solution)/shard_map/dot_general | solution.py:74
  73.8 3.9 %mul.310 = bf16[384,3840]{1,0:T(8,128)(2,1)S(1)} reshape(bf16[32,12,3840]{2,1,0:T(8,128)(2,1)} %get-tuple-element.41) | data formatting | bytes 5898240 | tf_op jit(solution)/shard_map/mul | solution.py:70
  77.7 3.2 %fusion.10 = f32[384,256]{1,0:T(8,128)} fusion(bf16[384,3840]{1,0:T(8,128)(2,1)S(1)} %mul.310, bf16[4,256,3840]{2,1,0:T(8,128)(2,1)} %copy-done.1), kind=kOutput, calls=%fused_computation.20 | convolution fusion | flops 754974720 | bytes 5308416 | tf_op jit(solution)/shard_map/dot_general | solution.py:74
  83.1 3.9 %mul.314 = bf16[384,3840]{1,0:T(8,128)(2,1)S(1)} reshape(bf16[32,12,3840]{2,1,0:T(8,128)(2,1)} %get-tuple-element.42) | data formatting | bytes 5898240 | tf_op jit(solution)/shard_map/mul | solution.py:70
  87.0 3.3 %fusion.6 = f32[384,256]{1,0:T(8,128)} fusion(bf16[384,3840]{1,0:T(8,128)(2,1)S(1)} %mul.314, bf16[4,256,3840]{2,1,0:T(8,128)(2,1)} %copy-done.1), kind=kOutput, calls=%fused_computation.16 | convolution fusion | flops 754974720 | bytes 5308416 | tf_op jit(solution)/shard_map/dot_general | solution.py:74
  95.9 3.5 %all-to-all-start.1 = ((bf16[128,4,768]{2,0,1:T(8,128)(2,1)}), bf16[128,4,768]{2,0,1:T(8,128)(2,1)S(1)}, u32[]{:S(2)}, u32[]{:S(2)}) async-start(bf16[128,4,768]{2,0,1:T(8,128)(2,1)} %copy.56), calls=%async_computation.1 | async-start | bytes 1572864 | tf_op jit(solution)/shard_map/all_to_all | solution.py:146
  102.6 8.4 %all-to-all-done.1 = bf16[128,4,768]{2,0,1:T(8,128)(2,1)S(1)} async-done(((bf16[128,4,768]{2,0,1:T(8,128)(2,1)}), bf16[128,4,768]{2,0,1:T(8,128)(2,1)S(1)}, u32[]{:S(2)}, u32[]{:S(2)}) %all-to-all-start.1) | async-done | bytes 786464 | tf_op jit(solution)/shard_map/all_to_all | solution.py:146
  115.1 3.5 %all-to-all-start.2 = ((bf16[4,128,768]{2,1,0:T(8,128)(2,1)}), bf16[4,128,768]{2,1,0:T(8,128)(2,1)S(1)}, u32[]{:S(2)}, u32[]{:S(2)}) async-start(bf16[4,128,768]{2,1,0:T(8,128)(2,1)} %bitcast.158), calls=%async_computation.2 | async-start | bytes 1572864 | tf_op jit(solution)/shard_map/all_to_all | solution.py:174
  118.9 2.8 %fusion.90 = f32[512,512]{1,0:T(8,128)} fusion(bf16[512,768]{1,0:T(8,128)(2,1)S(1)} %bitcast.153, bf16[512,768]{1,0:T(8,128)(2,1)} %copy-done.6), kind=kOutput, calls=%fused_computation.140 | convolution fusion | flops 402653184 | bytes 2621440 | tf_op jit(solution)/shard_map/dot_general | solution.py:160
  123.4 6.8 %all-to-all-done.2 = bf16[4,128,768]{2,1,0:T(8,128)(2,1)S(1)} async-done(((bf16[4,128,768]{2,1,0:T(8,128)(2,1)}), bf16[4,128,768]{2,1,0:T(8,128)(2,1)S(1)}, u32[]{:S(2)}, u32[]{:S(2)}) %all-to-all-start.2) | async-done | bytes 786464 | tf_op jit(solution)/shard_map/all_to_all | solution.py:174
  131.2 3.4 %slice_reduce_fusion.2 = (bf16[32,3072]{1,0:T(8,128)(2,1)S(1)}, bf16[32,3072]{1,0:T(8,128)(2,1)S(1)}, bf16[32,3072]{1,0:T(8,128)(2,1)S(1)}, bf16[32,3072]{1,0:T(8,128)(2,1)S(1)}) fusion(bf16[32,4,3072]{2,1,0:T(4,128)(2,1)S(1)} %reshape.284), kind=kLoop, calls=%fused_computation.71 | loop fusion | bytes 1572864 | tf_op jit(solution)/shard_map/slice | solution.py:107
  142.1 3.6 %collective-permute-start.2 = (f32[32,1280]{1,0:T(8,128)S(1)}, f32[32,1280]{1,0:T(8,128)S(1)}, u32[]{:S(2)}, u32[]{:S(2)}) collective-permute-start(f32[32,1280]{1,0:T(8,128)S(1)} %get-tuple-element.29), channel_id=1, source_target_pairs={{0,4},{4,8},{8,12},{12,16},{16,20},{20,24},{24,28},{1,5},{5,9},{9,... | collective-permute-start | bytes 491528 | tf_op jit(solution)/shard_map/ppermute | solution.py:18
  147.0 3.3 %collective-permute-done.2 = f32[32,1280]{1,0:T(8,128)S(1)} collective-permute-done((f32[32,1280]{1,0:T(8,128)S(1)}, f32[32,1280]{1,0:T(8,128)S(1)}, u32[]{:S(2)}, u32[]{:S(2)}) %collective-permute-start.2) | collective-permute-done | bytes 163872 | tf_op jit(solution)/shard_map/ppermute | solution.py:18
  153.9 5.2 %all-to-all-start.3 = ((f32[32,8,160]{2,0,1:T(8,128)}), f32[32,8,160]{2,0,1:T(8,128)S(1)}, u32[]{:S(2)}, u32[]{:S(2)}) async-start(f32[32,8,160]{2,0,1:T(8,128)} %copy.63), calls=%async_computation.3 | async-start | bytes 524288 | tf_op jit(solution)/shard_map/all_to_all | solution.py:180
  159.2 40.6 %psum.22 = f32[512]{0:T(512)} all-reduce(f32[512]{0:T(512)S(1)} %get-tuple-element.43), channel_id=1, replica_groups=mesh['band'=8,'rep'=4] {'band','rep'}, use_global_device_ids=true, to_apply=%region_10.11 | all-reduce | flops 512 | bytes 4096 | tf_op jit(solution)/shard_map/psum | solution.py:175
  201.9 58.7 %all-reduce.3.cloned.1.call-done = (f32[512,512]{1,0:T(8,128)}, f32[512,512]{1,0:T(8,128)}) async-done(((f32[512,512]{1,0:T(8,128)}, f32[512,512]{1,0:T(8,128)}), (f32[512,512]{1,0:T(8,128)}, f32[512,512]{1,0:T(8,128)})) %all-reduce.3.cloned.1.call-update) | async-done | bytes 2097168 | tf_op jit(solution)/shard_map/psum | solution.py:175
  (131 shorter events, 61.1 us)
Async XLA Ops:
  7.2 103.8 %copy-start = (bf16[512,512]{1,0:T(8,128)(2,1)S(1)}, bf16[512,512]{1,0:T(8,128)(2,1)}, u32[]{:S(2)}) copy-start(bf16[512,512]{1,0:T(8,128)(2,1)} %param.12) | copy-start | bytes 1572868
  10.8 28.9 %copy-start.18 = (s32[512,1]{0,1:T(1,128)}, s32[512,1]{0,1:T(1,128)S(1)}, u32[]{:S(2)}) copy-start(s32[512,1]{0,1:T(1,128)S(1)} %compare_select_fusion) | copy-start | bytes 6148
  14.6 14.9 %all-to-all-start = ((bf16[35,8,160]{2,0,1:T(8,128)(2,1)}), bf16[35,8,160]{2,0,1:T(8,128)(2,1)S(1)}, u32[]{:S(2)}, u32[]{:S(2)}) async-start(bf16[35,8,160]{2,0,1:T(8,128)(2,1)} %copy.50), calls=%async_computation | async-start | bytes 327680 | tf_op jit(solution)/shard_map/all_to_all | solution.py:139
  29.7 6.1 %collective-permute-start = (bf16[35,1280]{1,0:T(8,128)(2,1)S(1)}, bf16[35,1280]{1,0:T(8,128)(2,1)S(1)}, u32[]{:S(2)}, u32[]{:S(2)}) collective-permute-start(bf16[35,1280]{1,0:T(8,128)(2,1)S(1)} %all_to_all.42), channel_id=1, source_target_pairs={{0,4},{4,8},{8,12},{12,16},{16,20},{20,24},{24,28},{1,5},{5,9},{9,... | collective-permute-start | bytes 268808 | tf_op jit(solution)/shard_map/ppermute | solution.py:18
  32.6 6.6 %collective-permute-start.1 = (bf16[35,1280]{1,0:T(8,128)(2,1)S(1)}, bf16[35,1280]{1,0:T(8,128)(2,1)S(1)}, u32[]{:S(2)}, u32[]{:S(2)}) collective-permute-start(bf16[35,1280]{1,0:T(8,128)(2,1)S(1)} %all_to_all.42), channel_id=1, source_target_pairs={{4,0},{8,4},{12,8},{16,12},{20,16},{24,20},{28,24},{5,1},{9,5},{13... | collective-permute-start | bytes 268808 | tf_op jit(solution)/shard_map/ppermute | solution.py:20
  44.2 11.1 %copy-start.1 = (bf16[4,256,3840]{2,1,0:T(8,128)(2,1)}, bf16[4,256,3840]{2,1,0:T(8,128)(2,1)S(1)}, u32[]{:S(2)}) copy-start(bf16[4,256,3840]{2,1,0:T(8,128)(2,1)S(1)} %exponential_convert_fusion) | copy-start | bytes 23592964
  87.0 4.7 %copy-start.15 = (f32[12,256]{1,0:T(8,128)S(1)}, f32[12,256]{1,0:T(8,128)}, u32[]{:S(2)}) copy-start(f32[12,256]{1,0:T(8,128)} %fusion.8) | copy-start | bytes 36868
  87.0 4.7 %copy-start.16 = (f32[12,256]{1,0:T(8,128)S(1)}, f32[12,256]{1,0:T(8,128)}, u32[]{:S(2)}) copy-start(f32[12,256]{1,0:T(8,128)} %fusion.12) | copy-start | bytes 36868
  87.0 4.8 %copy-start.17 = (f32[12,256]{1,0:T(8,128)S(1)}, f32[12,256]{1,0:T(8,128)}, u32[]{:S(2)}) copy-start(f32[12,256]{1,0:T(8,128)} %fusion.16) | copy-start | bytes 36868
  94.9 4.5 %copy-start.4 = (bf16[512,3,256]{2,0,1:T(8,128)(2,1)S(1)}, bf16[512,3,256]{2,0,1:T(8,128)(2,1)}, u32[]{:S(2)}) copy-start(bf16[512,3,256]{2,0,1:T(8,128)(2,1)} %param.15) | copy-start | bytes 2359300
  95.9 15.1 %all-to-all-start.1 = ((bf16[128,4,768]{2,0,1:T(8,128)(2,1)}), bf16[128,4,768]{2,0,1:T(8,128)(2,1)S(1)}, u32[]{:S(2)}, u32[]{:S(2)}) async-start(bf16[128,4,768]{2,0,1:T(8,128)(2,1)} %copy.56), calls=%async_computation.1 | async-start | bytes 1572864 | tf_op jit(solution)/shard_map/all_to_all | solution.py:146
  100.8 10.2 %copy-start.21 = (f32[512]{0:T(512)S(1)}, f32[512]{0:T(512)}, u32[]{:S(2)}) copy-start(f32[512]{0:T(512)} %param.13) | copy-start | bytes 6148
  102.6 9.1 %copy-start.5 = (bf16[512,3,256]{0,2,1:T(8,128)(2,1)S(1)}, bf16[512,3,256]{0,2,1:T(8,128)(2,1)}, u32[]{:S(2)}) copy-start(bf16[512,3,256]{0,2,1:T(8,128)(2,1)} %copy.48) | copy-start | bytes 2359300
  102.6 9.1 %copy-start.20 = (bf16[512,512]{1,0:T(8,128)(2,1)S(1)}, bf16[512,512]{1,0:T(8,128)(2,1)}, u32[]{:S(2)}) copy-start(bf16[512,512]{1,0:T(8,128)(2,1)} %param.14) | copy-start | bytes 1572868
  115.1 15.1 %all-to-all-start.2 = ((bf16[4,128,768]{2,1,0:T(8,128)(2,1)}), bf16[4,128,768]{2,1,0:T(8,128)(2,1)S(1)}, u32[]{:S(2)}, u32[]{:S(2)}) async-start(bf16[4,128,768]{2,1,0:T(8,128)(2,1)} %bitcast.158), calls=%async_computation.2 | async-start | bytes 1572864 | tf_op jit(solution)/shard_map/all_to_all | solution.py:174
  118.6 141.9 %all-reduce.3.cloned.1.call-start = ((), (), s32[]{:S(2)}) async-start(), calls=%async_computation.4 | async-start | bytes 4194304 | tf_op jit(solution)/shard_map/psum | solution.py:175
  118.9 2.8 %copy-start.23 = (f32[768,512]{0,1:T(8,128)S(1)}, f32[768,512]{0,1:T(8,128)}, u32[]{:S(2)}) copy-start(f32[768,512]{0,1:T(8,128)} %copy-done.22) | copy-start | bytes 4718596
  130.8 3.7 %copy-start.14 = (f32[12,3840]{1,0:T(8,128)S(1)}, f32[12,3840]{1,0:T(8,128)}, u32[]{:S(2)}) copy-start(f32[12,3840]{1,0:T(8,128)} %get-tuple-element.31) | copy-start | bytes 552964
  131.1 8.8 %slice-start = ((s8[7864320]{0:T(1024)(128)(4,1)}), s8[3670016]{0:T(1024)(128)(4,1)S(1)}, s32[]{:S(2)}) async-start(s8[7864320]{0:T(1024)(128)(4,1)} %bitcast.149), calls=%async_computation.5 | async-start | bytes 7340032
  134.6 5.4 %slice-start.1 = ((s8[7864320]{0:T(1024)(128)(4,1)}), s8[4194304]{0:T(1024)(128)(4,1)S(1)}, s32[]{:S(2)}) async-start(s8[7864320]{0:T(1024)(128)(4,1)} %bitcast.149), calls=%async_computation.6 | async-start | bytes 8388608
  142.0 17.1 %copy-start.19 = (s32[512,1]{0,1:T(1,128)S(1)}, s32[512,1]{0,1:T(1,128)}, u32[]{:S(2)}) copy-start(s32[512,1]{0,1:T(1,128)} %copy-done.18) | copy-start | bytes 6148
  142.1 8.3 %collective-permute-start.2 = (f32[32,1280]{1,0:T(8,128)S(1)}, f32[32,1280]{1,0:T(8,128)S(1)}, u32[]{:S(2)}, u32[]{:S(2)}) collective-permute-start(f32[32,1280]{1,0:T(8,128)S(1)} %get-tuple-element.29), channel_id=1, source_target_pairs={{0,4},{4,8},{8,12},{12,16},{16,20},{20,24},{24,28},{1,5},{5,9},{9,... | collective-permute-start | bytes 491528 | tf_op jit(solution)/shard_map/ppermute | solution.py:18
  145.7 7.3 %collective-permute-start.3 = (f32[32,1280]{1,0:T(8,128)S(1)}, f32[32,1280]{1,0:T(8,128)S(1)}, u32[]{:S(2)}, u32[]{:S(2)}) collective-permute-start(f32[32,1280]{1,0:T(8,128)S(1)} %get-tuple-element.30), channel_id=1, source_target_pairs={{4,0},{8,4},{12,8},{16,12},{20,16},{24,20},{28,24},{5,1},{9,5},{13... | collective-permute-start | bytes 491528 | tf_op jit(solution)/shard_map/ppermute | solution.py:20
  153.9 45.9 %all-to-all-start.3 = ((f32[32,8,160]{2,0,1:T(8,128)}), f32[32,8,160]{2,0,1:T(8,128)S(1)}, u32[]{:S(2)}, u32[]{:S(2)}) async-start(f32[32,8,160]{2,0,1:T(8,128)} %copy.63), calls=%async_computation.3 | async-start | bytes 524288 | tf_op jit(solution)/shard_map/all_to_all | solution.py:180
  (11 other events, 24.3 us)
Sparse Core Ops, SparseCore 0:
  125.5 134.9 all-reduce.2
where the time goes:
time: 272 us; the launch traced here: 271 us
  waiting for transfers between devices  92.1 us (34%)
  local copies, waits for them, and re-layouts  42.5 us (16%)
  blocking collectives  40.6 us (15%)
  matrix products  33.1 us (12%)
  starting transfers between devices  28.8 us (11%)
  other arithmetic  18.9 us (7%)
  between operations  14.7 us (5%)
    psum x1, waiting for transfers between devices, on_device(): totals = lax.psum((first_sum, second_sum, bias_sum), ('band', 'rep'))  58.7 us
    psum x1, blocking collectives, on_device(): totals = lax.psum((first_sum, second_sum, bias_sum), ('band', 'rep'))  40.6 us
    mul x4, local copies, waits for them, and re-layouts, splat(): embedded[:, None, :] * row_kernel[level][None]  15.5 us
    dot_general x4, matrix products, splat(): lax.dot_general(weighted, column_kernel[level], (((1,), (1,)), ((), ())),...  13 us
    all_to_all x1, waiting for transfers between devices, on_device(): lax.all_to_all(features, 'rep', split_axis=1, concat_axis=0, tiled=True)  8.44 us
    another operation x4, local copies, waits for them, and re-layouts, splat(): splatted = jnp.stack(sums).reshape(levels, channels, lat_rows * columns)  7.83 us
    all_to_all x1, starting transfers between devices, on_device(): lax.all_to_all(outgoing, 'band', split_axis=1, concat_axis=1, tiled=True)  7.31 us
    dot_general x4, matrix products, spread_back(): jnp.dot(slab, column_kernel[level], preferred_element_type=jnp.float32)  7.24 us
  transfers between devices with their start and end apart: 9, of which 8 were waited for; matrix products, arithmetic and copies ran while one was open for 8% of the time, Pallas kernels for 0%

commit v1 on v0

--- a/solution.py
+++ b/solution.py
@@ -136,7 +136,15 @@
     rows = channels + 3
     whole = bands * capacity
     outgoing = jnp.zeros((rows, whole), jnp.bfloat16).at[:, owner * capacity + rank].set(packed)
-    arrived = lax.all_to_all(outgoing, "band", split_axis=1, concat_axis=1, tiled=True)
+    arrived = jnp.concatenate(
+        lax.all_to_all(
+            jnp.stack(jnp.split(outgoing, lax.psum(1, axis_name="band"), axis=1)),
+            concat_axis=0,
+            axis_name="band",
+            split_axis=0,
+        ),
+        axis=1,
+    )
     nearby = padded(arrived, (("band", 1),), whole)
     block = jnp.arange(3 * whole, dtype=jnp.int32) // whole
     geometry = nearby[channels:].astype(jnp.float32)

time: 272 us -> 272 us (level)
    unnamed x63 -> x72, local copies, waits for them, and re-layouts: 6.03 us -> 6.12 us
where the time goes in v1:
time: 272 us; the launch traced here: 271 us
  waiting for transfers between devices  92.7 us (34%)
  local copies, waits for them, and re-layouts  42.6 us (16%)
  blocking collectives  40.6 us (15%)
  matrix products  33.1 us (12%)
  starting transfers between devices  28.8 us (11%)
  other arithmetic  18.3 us (7%)
  between operations  14.7 us (5%)
    psum x1, waiting for transfers between devices, on_device(): totals = lax.psum((first_sum, second_sum, bias_sum), ('band', 'rep'))  58.7 us
    psum x1, blocking collectives, on_device(): totals = lax.psum((first_sum, second_sum, bias_sum), ('band', 'rep'))  40.6 us
    mul x4, local copies, waits for them, and re-layouts, splat(): embedded[:, None, :] * row_kernel[level][None]  15.5 us
    dot_general x4, matrix products, splat(): lax.dot_general(weighted, column_kernel[level], (((1,), (1,)), ((), ())),...  13 us
    all_to_all x1, waiting for transfers between devices, on_device(): lax.all_to_all(features, 'rep', split_axis=1, concat_axis=0, tiled=True)  8.44 us
    another operation x4, local copies, waits for them, and re-layouts, splat(): splatted = jnp.stack(sums).reshape(levels, channels, lat_rows * columns)  7.83 us
    all_to_all x1, waiting for transfers between devices, on_device(): lax.all_to_all(jnp.stack(jnp.split(outgoing, lax.psum(1, axis_name='band'...  7.51 us
    all_to_all x1, starting transfers between devices, on_device(): lax.all_to_all(jnp.stack(jnp.split(outgoing, lax.psum(1, axis_name='band'...  7.31 us
  transfers between devices with their start and end apart: 9, of which 8 were waited for; matrix products, arithmetic and copies ran while one was open for 8% of the time, Pallas kernels for 0%

profile of v1, /device:TPU:0, one launch (start us, length us, event | category | flops | bytes accessed | tf_op | source)
XLA Modules:
  0.0 270.9 jit_solution(7669994787686533595)
XLA Ops:
  14.8 7.3 %all-to-all-start = ((bf16[8,35,160]{2,1,0:T(8,128)(2,1)}), bf16[8,35,160]{2,1,0:T(8,128)(2,1)S(1)}, u32[]{:S(2)}, u32[]{:S(2)}) async-start(bf16[8,35,160]{2,1,0:T(8,128)(2,1)} %copy.86), calls=%async_computation | async-start | bytes 327680 | tf_op jit(solution)/shard_map/all_to_all | solution.py:140
  22.1 7.5 %all-to-all-done = bf16[8,35,160]{2,1,0:T(8,128)(2,1)S(1)} async-done(((bf16[8,35,160]{2,1,0:T(8,128)(2,1)}), bf16[8,35,160]{2,1,0:T(8,128)(2,1)S(1)}, u32[]{:S(2)}, u32[]{:S(2)}) %all-to-all-start) | async-done | bytes 89632 | tf_op jit(solution)/shard_map/all_to_all | solution.py:140
  36.0 3.3 %collective-permute-done.1 = bf16[35,1280]{1,0:T(8,128)(2,1)S(1)} collective-permute-done((bf16[35,1280]{1,0:T(8,128)(2,1)S(1)}, bf16[35,1280]{1,0:T(8,128)(2,1)S(1)}, u32[]{:S(2)}, u32[]{:S(2)}) %collective-permute-start.1) | collective-permute-done | bytes 89632 | tf_op jit(solution)/shard_map/ppermute | solution.py:20
  41.3 2.9 %exponential_convert_fusion = bf16[4,256,3840]{2,1,0:T(8,128)(2,1)S(1)} fusion(f32[4]{0:T(128)S(1)} %multiply_divide_fusion, f32[256,3840]{1,0:T(8,128)S(1)} %multiply_negate_fusion), kind=kLoop, calls=%fused_computation.2 | loop fusion | flops 7864320 | bytes 11796496 | tf_op jit(solution)/shard_map/convert_element_type | solution.py:57
  49.3 6.1 %broadcast_multiply_fusion.3 = (bf16[32,12,3840]{2,1,0:T(8,128)(2,1)}, bf16[32,12,3840]{2,1,0:T(8,128)(2,1)}, bf16[32,12,3840]{2,1,0:T(8,128)(2,1)}, bf16[32,12,3840]{2,1,0:T(8,128)(2,1)}) fusion(bf16[12,3840]{1,0:T(8,128)(2,1)S(1)} %copy-done.10, bf16[32,3840]{1,0:T(8,128)(2,1)S(1)} %slice.107, bf16[12,3840]{1,0:T(8,128)(2,1)S(1)} %copy-done.9, ...), kind=kLoop, calls=%fused_computation.33 | loop fusion | flops 5898240 | bytes 12410880 | tf_op jit(solution)/shard_map/mul | solution.py:70
  55.4 3.9 %mul.295 = bf16[384,3840]{1,0:T(8,128)(2,1)S(1)} reshape(bf16[32,12,3840]{2,1,0:T(8,128)(2,1)} %get-tuple-element.43) | data formatting | bytes 5898240 | tf_op jit(solution)/shard_map/mul | solution.py:70
  59.3 3.3 %fusion.18 = f32[384,256]{1,0:T(8,128)} fusion(bf16[384,3840]{1,0:T(8,128)(2,1)S(1)} %mul.295, bf16[4,256,3840]{2,1,0:T(8,128)(2,1)} %copy-done.1), kind=kOutput, calls=%fused_computation.28 | convolution fusion | flops 754974720 | bytes 5308416 | tf_op jit(solution)/shard_map/dot_general | solution.py:74
  64.7 3.9 %mul.306 = bf16[384,3840]{1,0:T(8,128)(2,1)S(1)} reshape(bf16[32,12,3840]{2,1,0:T(8,128)(2,1)} %get-tuple-element.44) | data formatting | bytes 5898240 | tf_op jit(solution)/shard_map/mul | solution.py:70
  68.6 3.3 %fusion.14 = f32[384,256]{1,0:T(8,128)} fusion(bf16[384,3840]{1,0:T(8,128)(2,1)S(1)} %mul.306, bf16[4,256,3840]{2,1,0:T(8,128)(2,1)} %copy-done.1), kind=kOutput, calls=%fused_computation.24 | convolution fusion | flops 754974720 | bytes 5308416 | tf_op jit(solution)/shard_map/dot_general | solution.py:74
  74.0 3.9 %mul.310 = bf16[384,3840]{1,0:T(8,128)(2,1)S(1)} reshape(bf16[32,12,3840]{2,1,0:T(8,128)(2,1)} %get-tuple-element.45) | data formatting | bytes 5898240 | tf_op jit(solution)/shard_map/mul | solution.py:70
  77.9 3.3 %fusion.10 = f32[384,256]{1,0:T(8,128)} fusion(bf16[384,3840]{1,0:T(8,128)(2,1)S(1)} %mul.310, bf16[4,256,3840]{2,1,0:T(8,128)(2,1)} %copy-done.1), kind=kOutput, calls=%fused_computation.20 | convolution fusion | flops 754974720 | bytes 5308416 | tf_op jit(solution)/shard_map/dot_general | solution.py:74
  83.3 3.9 %mul.314 = bf16[384,3840]{1,0:T(8,128)(2,1)S(1)} reshape(bf16[32,12,3840]{2,1,0:T(8,128)(2,1)} %get-tuple-element.46) | data formatting | bytes 5898240 | tf_op jit(solution)/shard_map/mul | solution.py:70
  87.2 3.3 %fusion.6 = f32[384,256]{1,0:T(8,128)} fusion(bf16[384,3840]{1,0:T(8,128)(2,1)S(1)} %mul.314, bf16[4,256,3840]{2,1,0:T(8,128)(2,1)} %copy-done.1), kind=kOutput, calls=%fused_computation.16 | convolution fusion | flops 754974720 | bytes 5308416 | tf_op jit(solution)/shard_map/dot_general | solution.py:74
  96.1 3.5 %all-to-all-start.1 = ((bf16[128,4,768]{2,0,1:T(8,128)(2,1)}), bf16[128,4,768]{2,0,1:T(8,128)(2,1)S(1)}, u32[]{:S(2)}, u32[]{:S(2)}) async-start(bf16[128,4,768]{2,0,1:T(8,128)(2,1)} %copy.92), calls=%async_computation.1 | async-start | bytes 1572864 | tf_op jit(solution)/shard_map/all_to_all | solution.py:154
  102.7 8.4 %all-to-all-done.1 = bf16[128,4,768]{2,0,1:T(8,128)(2,1)S(1)} async-done(((bf16[128,4,768]{2,0,1:T(8,128)(2,1)}), bf16[128,4,768]{2,0,1:T(8,128)(2,1)S(1)}, u32[]{:S(2)}, u32[]{:S(2)}) %all-to-all-start.1) | async-done | bytes 786464 | tf_op jit(solution)/shard_map/all_to_all | solution.py:154
  115.3 3.5 %all-to-all-start.2 = ((bf16[4,128,768]{2,1,0:T(8,128)(2,1)}), bf16[4,128,768]{2,1,0:T(8,128)(2,1)S(1)}, u32[]{:S(2)}, u32[]{:S(2)}) async-start(bf16[4,128,768]{2,1,0:T(8,128)(2,1)} %bitcast.189), calls=%async_computation.2 | async-start | bytes 1572864 | tf_op jit(solution)/shard_map/all_to_all | solution.py:182
  119.1 2.8 %fusion.98 = f32[512,512]{1,0:T(8,128)} fusion(bf16[512,768]{1,0:T(8,128)(2,1)S(1)} %bitcast.185, bf16[512,768]{1,0:T(8,128)(2,1)} %copy-done.6), kind=kOutput, calls=%fused_computation.156 | convolution fusion | flops 402653184 | bytes 2621440 | tf_op jit(solution)/shard_map/dot_general | solution.py:168
  123.5 6.8 %all-to-all-done.2 = bf16[4,128,768]{2,1,0:T(8,128)(2,1)S(1)} async-done(((bf16[4,128,768]{2,1,0:T(8,128)(2,1)}), bf16[4,128,768]{2,1,0:T(8,128)(2,1)S(1)}, u32[]{:S(2)}, u32[]{:S(2)}) %all-to-all-start.2) | async-done | bytes 786464 | tf_op jit(solution)/shard_map/all_to_all | solution.py:182
  131.3 3.4 %slice_reduce_fusion.2 = (bf16[32,3072]{1,0:T(8,128)(2,1)S(1)}, bf16[32,3072]{1,0:T(8,128)(2,1)S(1)}, bf16[32,3072]{1,0:T(8,128)(2,1)S(1)}, bf16[32,3072]{1,0:T(8,128)(2,1)S(1)}) fusion(bf16[32,4,3072]{2,1,0:T(4,128)(2,1)S(1)} %reshape.290), kind=kLoop, calls=%fused_computation.71 | loop fusion | bytes 1572864 | tf_op jit(solution)/shard_map/slice | solution.py:107
  142.2 3.6 %collective-permute-start.2 = (f32[32,1280]{1,0:T(8,128)S(1)}, f32[32,1280]{1,0:T(8,128)S(1)}, u32[]{:S(2)}, u32[]{:S(2)}) collective-permute-start(f32[32,1280]{1,0:T(8,128)S(1)} %get-tuple-element.33), channel_id=1, source_target_pairs={{0,4},{4,8},{8,12},{12,16},{16,20},{20,24},{24,28},{1,5},{5,9},{9,... | collective-permute-start | bytes 491528 | tf_op jit(solution)/shard_map/ppermute | solution.py:18
  147.2 3.3 %collective-permute-done.2 = f32[32,1280]{1,0:T(8,128)S(1)} collective-permute-done((f32[32,1280]{1,0:T(8,128)S(1)}, f32[32,1280]{1,0:T(8,128)S(1)}, u32[]{:S(2)}, u32[]{:S(2)}) %collective-permute-start.2) | collective-permute-done | bytes 163872 | tf_op jit(solution)/shard_map/ppermute | solution.py:18
  154.1 5.2 %all-to-all-start.3 = ((f32[32,8,160]{2,0,1:T(8,128)}), f32[32,8,160]{2,0,1:T(8,128)S(1)}, u32[]{:S(2)}, u32[]{:S(2)}) async-start(f32[32,8,160]{2,0,1:T(8,128)} %copy.99), calls=%async_computation.3 | async-start | bytes 524288 | tf_op jit(solution)/shard_map/all_to_all | solution.py:188
  159.3 40.6 %psum.22 = f32[512]{0:T(512)} all-reduce(f32[512]{0:T(512)S(1)} %get-tuple-element.47), channel_id=1, replica_groups=mesh['band'=8,'rep'=4] {'band','rep'}, use_global_device_ids=true, to_apply=%region_10.11 | all-reduce | flops 512 | bytes 4096 | tf_op jit(solution)/shard_map/psum | solution.py:183
  202.0 58.7 %all-reduce.3.cloned.1.call-done = (f32[512,512]{1,0:T(8,128)}, f32[512,512]{1,0:T(8,128)}) async-done(((f32[512,512]{1,0:T(8,128)}, f32[512,512]{1,0:T(8,128)}), (f32[512,512]{1,0:T(8,128)}, f32[512,512]{1,0:T(8,128)})) %all-reduce.3.cloned.1.call-update) | async-done | bytes 2097168 | tf_op jit(solution)/shard_map/psum | solution.py:183
  (141 shorter events, 60.5 us)
Async XLA Ops:
  7.2 104.0 %copy-start = (bf16[512,512]{1,0:T(8,128)(2,1)S(1)}, bf16[512,512]{1,0:T(8,128)(2,1)}, u32[]{:S(2)}) copy-start(bf16[512,512]{1,0:T(8,128)(2,1)} %param.12) | copy-start | bytes 1572868
  7.2 14.9 %copy-start.22 = (f32[4]{0:T(128)S(1)}, f32[4]{0:T(128)}, u32[]{:S(2)}) copy-start(f32[4]{0:T(128)} %param.11) | copy-start | bytes 52
  14.8 14.9 %all-to-all-start = ((bf16[8,35,160]{2,1,0:T(8,128)(2,1)}), bf16[8,35,160]{2,1,0:T(8,128)(2,1)S(1)}, u32[]{:S(2)}, u32[]{:S(2)}) async-start(bf16[8,35,160]{2,1,0:T(8,128)(2,1)} %copy.86), calls=%async_computation | async-start | bytes 327680 | tf_op jit(solution)/shard_map/all_to_all | solution.py:140
  29.9 6.1 %collective-permute-start = (bf16[35,1280]{1,0:T(8,128)(2,1)S(1)}, bf16[35,1280]{1,0:T(8,128)(2,1)S(1)}, u32[]{:S(2)}, u32[]{:S(2)}) collective-permute-start(bf16[35,1280]{1,0:T(8,128)(2,1)S(1)} %reshape.289), channel_id=1, source_target_pairs={{0,4},{4,8},{8,12},{12,16},{16,20},{20,24},{24,28},{1,5},{5,9},{9,... | collective-permute-start | bytes 268808 | tf_op jit(solution)/shard_map/ppermute | solution.py:18
  32.7 6.6 %collective-permute-start.1 = (bf16[35,1280]{1,0:T(8,128)(2,1)S(1)}, bf16[35,1280]{1,0:T(8,128)(2,1)S(1)}, u32[]{:S(2)}, u32[]{:S(2)}) collective-permute-start(bf16[35,1280]{1,0:T(8,128)(2,1)S(1)} %reshape.289), channel_id=1, source_target_pairs={{4,0},{8,4},{12,8},{16,12},{20,16},{24,20},{28,24},{5,1},{9,5},{13... | collective-permute-start | bytes 268808 | tf_op jit(solution)/shard_map/ppermute | solution.py:20
  44.3 11.1 %copy-start.1 = (bf16[4,256,3840]{2,1,0:T(8,128)(2,1)}, bf16[4,256,3840]{2,1,0:T(8,128)(2,1)S(1)}, u32[]{:S(2)}) copy-start(bf16[4,256,3840]{2,1,0:T(8,128)(2,1)S(1)} %exponential_convert_fusion) | copy-start | bytes 23592964
  87.1 4.7 %copy-start.15 = (f32[12,256]{1,0:T(8,128)S(1)}, f32[12,256]{1,0:T(8,128)}, u32[]{:S(2)}) copy-start(f32[12,256]{1,0:T(8,128)} %fusion.8) | copy-start | bytes 36868
  87.2 4.7 %copy-start.16 = (f32[12,256]{1,0:T(8,128)S(1)}, f32[12,256]{1,0:T(8,128)}, u32[]{:S(2)}) copy-start(f32[12,256]{1,0:T(8,128)} %fusion.12) | copy-start | bytes 36868
  87.2 4.8 %copy-start.17 = (f32[12,256]{1,0:T(8,128)S(1)}, f32[12,256]{1,0:T(8,128)}, u32[]{:S(2)}) copy-start(f32[12,256]{1,0:T(8,128)} %fusion.16) | copy-start | bytes 36868
  95.1 4.5 %copy-start.4 = (bf16[512,3,256]{2,0,1:T(8,128)(2,1)S(1)}, bf16[512,3,256]{2,0,1:T(8,128)(2,1)}, u32[]{:S(2)}) copy-start(bf16[512,3,256]{2,0,1:T(8,128)(2,1)} %param.15) | copy-start | bytes 2359300
  96.1 15.1 %all-to-all-start.1 = ((bf16[128,4,768]{2,0,1:T(8,128)(2,1)}), bf16[128,4,768]{2,0,1:T(8,128)(2,1)S(1)}, u32[]{:S(2)}, u32[]{:S(2)}) async-start(bf16[128,4,768]{2,0,1:T(8,128)(2,1)} %copy.92), calls=%async_computation.1 | async-start | bytes 1572864 | tf_op jit(solution)/shard_map/all_to_all | solution.py:154
  101.0 10.2 %copy-start.21 = (f32[512]{0:T(512)S(1)}, f32[512]{0:T(512)}, u32[]{:S(2)}) copy-start(f32[512]{0:T(512)} %param.13) | copy-start | bytes 6148
  102.7 9.1 %copy-start.5 = (bf16[512,3,256]{0,2,1:T(8,128)(2,1)S(1)}, bf16[512,3,256]{0,2,1:T(8,128)(2,1)}, u32[]{:S(2)}) copy-start(bf16[512,3,256]{0,2,1:T(8,128)(2,1)} %copy.84) | copy-start | bytes 2359300
  102.7 9.1 %copy-start.20 = (bf16[512,512]{1,0:T(8,128)(2,1)S(1)}, bf16[512,512]{1,0:T(8,128)(2,1)}, u32[]{:S(2)}) copy-start(bf16[512,512]{1,0:T(8,128)(2,1)} %param.14) | copy-start | bytes 1572868
  115.3 15.1 %all-to-all-start.2 = ((bf16[4,128,768]{2,1,0:T(8,128)(2,1)}), bf16[4,128,768]{2,1,0:T(8,128)(2,1)S(1)}, u32[]{:S(2)}, u32[]{:S(2)}) async-start(bf16[4,128,768]{2,1,0:T(8,128)(2,1)} %bitcast.189), calls=%async_computation.2 | async-start | bytes 1572864 | tf_op jit(solution)/shard_map/all_to_all | solution.py:182
  118.8 141.9 %all-reduce.3.cloned.1.call-start = ((), (), s32[]{:S(2)}) async-start(), calls=%async_computation.4 | async-start | bytes 4194304 | tf_op jit(solution)/shard_map/psum | solution.py:183
  119.0 2.8 %copy-start.24 = (f32[768,512]{0,1:T(8,128)S(1)}, f32[768,512]{0,1:T(8,128)}, u32[]{:S(2)}) copy-start(f32[768,512]{0,1:T(8,128)} %copy-done.23) | copy-start | bytes 4718596
  131.0 3.7 %copy-start.14 = (f32[12,3840]{1,0:T(8,128)S(1)}, f32[12,3840]{1,0:T(8,128)}, u32[]{:S(2)}) copy-start(f32[12,3840]{1,0:T(8,128)} %get-tuple-element.35) | copy-start | bytes 552964
  131.3 8.8 %slice-start = ((s8[7864320]{0:T(1024)(128)(4,1)}), s8[3670016]{0:T(1024)(128)(4,1)S(1)}, s32[]{:S(2)}) async-start(s8[7864320]{0:T(1024)(128)(4,1)} %bitcast.181), calls=%async_computation.5 | async-start | bytes 7340032
  134.7 5.4 %slice-start.1 = ((s8[7864320]{0:T(1024)(128)(4,1)}), s8[4194304]{0:T(1024)(128)(4,1)S(1)}, s32[]{:S(2)}) async-start(s8[7864320]{0:T(1024)(128)(4,1)} %bitcast.181), calls=%async_computation.6 | async-start | bytes 8388608
  142.2 17.1 %copy-start.19 = (s32[512,1]{0,1:T(1,128)S(1)}, s32[512,1]{0,1:T(1,128)}, u32[]{:S(2)}) copy-start(s32[512,1]{0,1:T(1,128)} %copy-done.18) | copy-start | bytes 6148
  142.2 8.3 %collective-permute-start.2 = (f32[32,1280]{1,0:T(8,128)S(1)}, f32[32,1280]{1,0:T(8,128)S(1)}, u32[]{:S(2)}, u32[]{:S(2)}) collective-permute-start(f32[32,1280]{1,0:T(8,128)S(1)} %get-tuple-element.33), channel_id=1, source_target_pairs={{0,4},{4,8},{8,12},{12,16},{16,20},{20,24},{24,28},{1,5},{5,9},{9,... | collective-permute-start | bytes 491528 | tf_op jit(solution)/shard_map/ppermute | solution.py:18
  145.9 7.2 %collective-permute-start.3 = (f32[32,1280]{1,0:T(8,128)S(1)}, f32[32,1280]{1,0:T(8,128)S(1)}, u32[]{:S(2)}, u32[]{:S(2)}) collective-permute-start(f32[32,1280]{1,0:T(8,128)S(1)} %get-tuple-element.34), channel_id=1, source_target_pairs={{4,0},{8,4},{12,8},{16,12},{20,16},{24,20},{28,24},{5,1},{9,5},{13... | collective-permute-start | bytes 491528 | tf_op jit(solution)/shard_map/ppermute | solution.py:20
  154.1 45.9 %all-to-all-start.3 = ((f32[32,8,160]{2,0,1:T(8,128)}), f32[32,8,160]{2,0,1:T(8,128)S(1)}, u32[]{:S(2)}, u32[]{:S(2)}) async-start(f32[32,8,160]{2,0,1:T(8,128)} %copy.99), calls=%async_computation.3 | async-start | bytes 524288 | tf_op jit(solution)/shard_map/all_to_all | solution.py:188
  (12 other events, 25.4 us)
Sparse Core Ops, SparseCore 0:
  125.7 134.9 all-reduce.2
